TPU v7x, 256 devices: a whole 4x4x8 slice. The times are simulated.
256 devices in a mesh: gy: 8 (over y, core), gx: 32 (over z, x).
Axes of the slice: x: 4, y: 4, z: 8, core: 2. Of those that a mesh axis runs over, the one named last changes fastest.
Arguments:
- ramp: int32 [32], replicated, may hold values from 0 to 7
- seed_mask: int32 [1024, 8192], P('gy', 'gx'), may hold values 0 or 1
- noise: float32 [2, 1024, 8192], P(None, 'gy', 'gx'), may hold values from -4 to 4
Outputs:
- filtered: float32 [32, 2, 1024, 8192], P(None, None, 'gy', 'gx')
- filter_matrix: float32 [32, 32], replicated
All inputs are finite; a program needn't handle non-finite values. No bound on the sum of `seed_mask` on one device may be relied on, other than what follows from the above.
Results may differ from a plain program's by a relative error of at most 0.0045.
Values sent between devices are 32-bit elements; how exact they have to be, the bound alone decides.
A program may use at most 64 MiB of HBM per device.

v0:
```python
import jax
import jax.numpy as jnp
from jax import lax
from jax.sharding import PartitionSpec as P

SNAPS = 32
RATES = 8


def padded_2(block, sides, width):
    for axis, dim in sides:
        count = lax.axis_size(axis)
        forward = [(i, i + 1) for i in range(count - 1)]
        forward.append((count - 1, 0))
        backward = [(target, source) for source, target in forward]
        low = lax.ppermute(
            lax.slice_in_dim(block, block.shape[dim] - width, None, axis=dim), axis, forward
        )
        high = lax.ppermute(lax.slice_in_dim(block, 0, width, axis=dim), axis, backward)
        block = jnp.concatenate([low, block, high], axis=dim)
    return block


def advance(padded, rate):
    center = padded[:, 1:-1, 1:-1]
    laplace = (
        padded[:, :-2, 1:-1]
        + padded[:, 2:, 1:-1]
        + padded[:, 1:-1, :-2]
        + padded[:, 1:-1, 2:]
        - 4.0 * center
    )
    u_now = center[0]
    v_now = center[1]
    react = u_now * v_now * v_now
    u_new = u_now + 0.2 * laplace[0] - react + rate * (1.0 - u_now)
    v_new = v_now + 0.1 * laplace[1] + react - (rate + 0.06) * v_now
    return jnp.stack([u_new, v_new])


def local(ramp, seed_mask, noise):
    rows = seed_mask.shape[0]
    total_rows = rows * lax.axis_size("gy")
    table = 0.01 + 0.008 * jnp.arange(RATES, dtype=jnp.float32)
    onehot = (ramp[:, None] == jnp.arange(RATES, dtype=jnp.int32)[None, :]).astype(jnp.float32)
    rates = jnp.sum(onehot * table[None, :], axis=1)
    row_pos = (lax.axis_index("gy") * rows + jnp.arange(rows, dtype=jnp.int32)).astype(jnp.float32)
    amplitude = (0.5 + 1.5 * (row_pos + 0.5) / total_rows)[:, None]
    mask = seed_mask.astype(jnp.float32)
    u_start = 1.0 - 0.5 * mask + 0.1 * amplitude * noise[0]
    v_start = 0.25 * mask + 0.1 * amplitude * noise[1]
    state = jnp.stack([u_start, v_start])

    def one_step(current, rate):
        padded = padded_2(current, (("gy", 1), ("gx", 2)), 1)
        fresh = advance(padded, rate)
        return (fresh, fresh)

    final, snaps = lax.scan(one_step, state, rates)
    average = jnp.mean(snaps, axis=0)
    centered = snaps - average[None]
    flat = centered.reshape(SNAPS, -1)
    local_gram = jnp.dot(
        flat, flat.T, precision=lax.Precision.HIGHEST, preferred_element_type=jnp.float32
    )
    gram = lax.psum(local_gram, ("gy", "gx"))
    shift_val = 0.01 * jnp.trace(gram) / SNAPS
    shifted = gram + shift_val * jnp.eye(SNAPS, dtype=jnp.float32)
    factor = jnp.linalg.cholesky(shifted)
    forward = lax.linalg.triangular_solve(factor, gram, left_side=True, lower=True)
    filter_matrix = lax.linalg.triangular_solve(
        factor, forward, left_side=True, lower=True, transpose_a=True
    )
    filtered = jnp.dot(
        filter_matrix.T, flat, precision=lax.Precision.HIGHEST, preferred_element_type=jnp.float32
    )
    return (filtered.reshape(centered.shape), filter_matrix)


def solution(mesh):
    return jax.shard_map(
        local,
        mesh=mesh,
        in_specs=(P(), P("gy", "gx"), P(None, "gy", "gx")),
        out_specs=(P(None, None, "gy", "gx"), P()),
        check_vma=False,
    )
```

profile of v0, /device:TPU:1, one launch (start us, length us, event | category | flops | bytes accessed | tf_op | source)
XLA Modules:
  0.0 607.9 jit_solution(7404693475670803302)
XLA Ops:
  2.6 478.3 %while.12 = (s32[]{:T(128)}, f32[2,128,256]{2,1,0:T(8,128)S(1)}, f32[32,2,128,256]{3,2,1,0:T(8,128)}, f32[32]{0:T(128)S(1)}, s32[]{:T(128)}, /*index=5*/f32[]{:T(128)}) while((s32[]{:T(128)}, f32[2,128,256]{2,1,0:T(8,128)S(1)}, f32[32,2,128,256]{3,2,1,0:T(8,128)}, f32[32]{0:T(128)S(1)}, s32[]{:T(128)}, /*index=5*/f32[]{:T(128)}) %tuple.38), condition=%wide.region_2.3_spmd, body=%wide.region_1.2_spmd.sunk | while | flops 1476611 | bytes 2673137 | solution.py:59
  7.3 7.8 %collective-permute-start.2 = (f32[2,130,1]{2,1,0:T(8,128)S(1)}, f32[2,130,1]{2,1,0:T(8,128)S(1)}, u32[]{:S(2)}, u32[]{:S(2)}) collective-permute-start(f32[2,130,1]{2,1,0:T(8,128)S(1)} %get-tuple-element.84), channel_id=1, source_target_pairs={{1,0},{2,1},{3,2},{4,3},{5,4},{6,5},{7,6},{8,7},{9,8},{10,9},{11,1... | collective-permute-start | bytes 3128 | tf_op jit(solution)/shard_map/while/body/eval_jaxpr/ppermute | solution.py:19
  17.2 5.2 collective-permute-done.3
  24.2 5.0 collective-permute-start
  34.4 3.4 collective-permute-done.3
  39.6 4.7 collective-permute-start
  49.5 3.4 collective-permute-done.3
  54.7 4.5 collective-permute-start
  64.5 3.4 collective-permute-done.3
  69.7 4.3 collective-permute-start
  79.2 3.4 collective-permute-done.3
  84.4 4.2 collective-permute-start
  93.9 3.4 collective-permute-done.3
  99.1 4.2 collective-permute-start
  108.6 3.4 collective-permute-done.3
  113.8 4.2 collective-permute-start
  123.3 3.4 collective-permute-done.3
  128.5 4.2 collective-permute-start
  138.0 3.4 collective-permute-done.3
  143.2 4.2 collective-permute-start
  152.7 3.4 collective-permute-done.3
  157.8 4.2 collective-permute-start
  167.3 3.4 collective-permute-done.3
  172.5 4.2 collective-permute-start
  182.0 3.4 collective-permute-done.3
  187.2 4.2 collective-permute-start
  196.7 3.4 collective-permute-done.3
  201.9 4.2 collective-permute-start
  211.4 3.4 collective-permute-done.3
  216.6 4.2 collective-permute-start
  226.1 3.4 collective-permute-done.3
  231.2 4.2 collective-permute-start
  240.7 3.4 collective-permute-done.3
  245.9 4.2 collective-permute-start
  255.4 3.4 collective-permute-done.3
  260.6 4.2 collective-permute-start
  270.1 3.4 collective-permute-done.3
  275.3 4.2 collective-permute-start
  284.8 3.4 collective-permute-done.3
  290.0 4.2 collective-permute-start
  304.7 4.2 collective-permute-start
  314.2 3.4 collective-permute-done.3
  319.3 4.2 collective-permute-start
  334.0 4.2 collective-permute-start
  348.7 4.2 collective-permute-start
  358.2 3.4 collective-permute-done.3
  363.4 4.2 collective-permute-start
  372.9 3.4 collective-permute-done.3
  378.1 4.2 collective-permute-start
  392.7 4.2 collective-permute-start
  407.4 4.2 collective-permute-start
  416.9 3.4 collective-permute-done.3
  422.1 4.2 collective-permute-start
  436.8 4.2 collective-permute-start
  451.5 4.2 collective-permute-start
  466.2 4.2 collective-permute-start
  475.7 3.4 collective-permute-done.3
  480.8 3.9 reduce_sum.29
  484.8 4.0 broadcast_subtract_fusion
  488.8 10.9 %fusion.14 = f32[32,32]{1,0:T(8,128)S(1)} fusion(f32[32,2,128,256]{3,2,1,0:T(8,128)S(1)} %broadcast_subtract_fusion), kind=kOutput, calls=%fused_computation.29 | convolution fusion | flops 805306368 | bytes 8392704 | tf_op jit(solution)/shard_map/dot_general | solution.py:63
  499.7 74.7 %psum.7 = f32[32,32]{1,0:T(8,128)S(1)} all-reduce(f32[32,32]{1,0:T(8,128)S(1)} %fusion.14), channel_id=1, replica_groups=mesh['gy'=8,'gx'=32] {'gy','gx'}, use_global_device_ids=true, to_apply=%region_4.5 | all-reduce | flops 1024 | bytes 8192 | tf_op jit(solution)/shard_map/psum | solution.py:66
  582.8 4.0 fusion.32
  586.9 12.7 %fusion.10 = f32[32,2,128,256]{3,0,2,1:T(8,128)S(1)} fusion(f32[2,128,256,32]{2,1,0,3:T(8,128)S(1)} %fusion.32, f32[32,32]{1,0:T(8,128)S(1)} %fusion.23), kind=kOutput, calls=%fused_computation.24 | convolution fusion | flops 805306368 | bytes 16781312 | tf_op jit(solution)/shard_map/dot_general | solution.py:74
  599.6 8.3 %copy.21 = f32[32,2,128,256]{3,2,1,0:T(8,128)} copy(f32[32,2,128,256]{3,0,2,1:T(8,128)S(1)} %fusion.10) | data formatting | bytes 16777216
  (444 shorter events, 240.6 us)
Async XLA Ops:
  7.3 9.9 %collective-permute-start.2 = (f32[2,130,1]{2,1,0:T(8,128)S(1)}, f32[2,130,1]{2,1,0:T(8,128)S(1)}, u32[]{:S(2)}, u32[]{:S(2)}) collective-permute-start(f32[2,130,1]{2,1,0:T(8,128)S(1)} %get-tuple-element.84), channel_id=1, source_target_pairs={{1,0},{2,1},{3,2},{4,3},{5,4},{6,5},{7,6},{8,7},{9,8},{10,9},{11,1... | collective-permute-start | bytes 3128 | tf_op jit(solution)/shard_map/while/body/eval_jaxpr/ppermute | solution.py:19
  15.2 7.2 %collective-permute-start.3 = (f32[2,130,1]{2,1,0:T(8,128)S(1)}, f32[2,130,1]{2,1,0:T(8,128)S(1)}, u32[]{:S(2)}, u32[]{:S(2)}) collective-permute-start(f32[2,130,1]{2,1,0:T(8,128)S(1)} %get-tuple-element.85), channel_id=1, source_target_pairs={{0,1},{1,2},{2,3},{3,4},{4,5},{5,6},{6,7},{7,8},{8,9},{9,10},{10,1... | collective-permute-start | bytes 3128 | tf_op jit(solution)/shard_map/while/body/eval_jaxpr/ppermute | solution.py:16
  24.2 5.8 collective-permute-start
  30.5 7.3 %collective-permute-start.3 = (f32[2,130,1]{2,1,0:T(8,128)S(1)}, f32[2,130,1]{2,1,0:T(8,128)S(1)}, u32[]{:S(2)}, u32[]{:S(2)}) collective-permute-start(f32[2,130,1]{2,1,0:T(8,128)S(1)} %get-tuple-element.85), channel_id=1, source_target_pairs={{0,1},{1,2},{2,3},{3,4},{4,5},{5,6},{6,7},{7,8},{8,9},{9,10},{10,1... | collective-permute-start | bytes 3128 | tf_op jit(solution)/shard_map/while/body/eval_jaxpr/ppermute | solution.py:16
  39.6 5.5 collective-permute-start
  45.7 7.3 %collective-permute-start.3 = (f32[2,130,1]{2,1,0:T(8,128)S(1)}, f32[2,130,1]{2,1,0:T(8,128)S(1)}, u32[]{:S(2)}, u32[]{:S(2)}) collective-permute-start(f32[2,130,1]{2,1,0:T(8,128)S(1)} %get-tuple-element.85), channel_id=1, source_target_pairs={{0,1},{1,2},{2,3},{3,4},{4,5},{5,6},{6,7},{7,8},{8,9},{9,10},{10,1... | collective-permute-start | bytes 3128 | tf_op jit(solution)/shard_map/while/body/eval_jaxpr/ppermute | solution.py:16
  54.7 5.3 collective-permute-start
  60.6 7.3 %collective-permute-start.3 = (f32[2,130,1]{2,1,0:T(8,128)S(1)}, f32[2,130,1]{2,1,0:T(8,128)S(1)}, u32[]{:S(2)}, u32[]{:S(2)}) collective-permute-start(f32[2,130,1]{2,1,0:T(8,128)S(1)} %get-tuple-element.85), channel_id=1, source_target_pairs={{0,1},{1,2},{2,3},{3,4},{4,5},{5,6},{6,7},{7,8},{8,9},{9,10},{10,1... | collective-permute-start | bytes 3128 | tf_op jit(solution)/shard_map/while/body/eval_jaxpr/ppermute | solution.py:16
  69.7 5.1 collective-permute-start
  75.3 7.3 %collective-permute-start.3 = (f32[2,130,1]{2,1,0:T(8,128)S(1)}, f32[2,130,1]{2,1,0:T(8,128)S(1)}, u32[]{:S(2)}, u32[]{:S(2)}) collective-permute-start(f32[2,130,1]{2,1,0:T(8,128)S(1)} %get-tuple-element.85), channel_id=1, source_target_pairs={{0,1},{1,2},{2,3},{3,4},{4,5},{5,6},{6,7},{7,8},{8,9},{9,10},{10,1... | collective-permute-start | bytes 3128 | tf_op jit(solution)/shard_map/while/body/eval_jaxpr/ppermute | solution.py:16
  84.4 5.0 collective-permute-start
  90.0 7.3 %collective-permute-start.3 = (f32[2,130,1]{2,1,0:T(8,128)S(1)}, f32[2,130,1]{2,1,0:T(8,128)S(1)}, u32[]{:S(2)}, u32[]{:S(2)}) collective-permute-start(f32[2,130,1]{2,1,0:T(8,128)S(1)} %get-tuple-element.85), channel_id=1, source_target_pairs={{0,1},{1,2},{2,3},{3,4},{4,5},{5,6},{6,7},{7,8},{8,9},{9,10},{10,1... | collective-permute-start | bytes 3128 | tf_op jit(solution)/shard_map/while/body/eval_jaxpr/ppermute | solution.py:16
  99.1 5.0 collective-permute-start
  104.7 7.3 %collective-permute-start.3 = (f32[2,130,1]{2,1,0:T(8,128)S(1)}, f32[2,130,1]{2,1,0:T(8,128)S(1)}, u32[]{:S(2)}, u32[]{:S(2)}) collective-permute-start(f32[2,130,1]{2,1,0:T(8,128)S(1)} %get-tuple-element.85), channel_id=1, source_target_pairs={{0,1},{1,2},{2,3},{3,4},{4,5},{5,6},{6,7},{7,8},{8,9},{9,10},{10,1... | collective-permute-start | bytes 3128 | tf_op jit(solution)/shard_map/while/body/eval_jaxpr/ppermute | solution.py:16
  113.8 5.0 collective-permute-start
  119.4 7.3 %collective-permute-start.3 = (f32[2,130,1]{2,1,0:T(8,128)S(1)}, f32[2,130,1]{2,1,0:T(8,128)S(1)}, u32[]{:S(2)}, u32[]{:S(2)}) collective-permute-start(f32[2,130,1]{2,1,0:T(8,128)S(1)} %get-tuple-element.85), channel_id=1, source_target_pairs={{0,1},{1,2},{2,3},{3,4},{4,5},{5,6},{6,7},{7,8},{8,9},{9,10},{10,1... | collective-permute-start | bytes 3128 | tf_op jit(solution)/shard_map/while/body/eval_jaxpr/ppermute | solution.py:16
  128.5 5.0 collective-permute-start
  134.1 7.3 %collective-permute-start.3 = (f32[2,130,1]{2,1,0:T(8,128)S(1)}, f32[2,130,1]{2,1,0:T(8,128)S(1)}, u32[]{:S(2)}, u32[]{:S(2)}) collective-permute-start(f32[2,130,1]{2,1,0:T(8,128)S(1)} %get-tuple-element.85), channel_id=1, source_target_pairs={{0,1},{1,2},{2,3},{3,4},{4,5},{5,6},{6,7},{7,8},{8,9},{9,10},{10,1... | collective-permute-start | bytes 3128 | tf_op jit(solution)/shard_map/while/body/eval_jaxpr/ppermute | solution.py:16
  143.2 5.0 collective-permute-start
  148.8 7.3 %collective-permute-start.3 = (f32[2,130,1]{2,1,0:T(8,128)S(1)}, f32[2,130,1]{2,1,0:T(8,128)S(1)}, u32[]{:S(2)}, u32[]{:S(2)}) collective-permute-start(f32[2,130,1]{2,1,0:T(8,128)S(1)} %get-tuple-element.85), channel_id=1, source_target_pairs={{0,1},{1,2},{2,3},{3,4},{4,5},{5,6},{6,7},{7,8},{8,9},{9,10},{10,1... | collective-permute-start | bytes 3128 | tf_op jit(solution)/shard_map/while/body/eval_jaxpr/ppermute | solution.py:16
  157.8 5.0 collective-permute-start
  163.4 7.3 %collective-permute-start.3 = (f32[2,130,1]{2,1,0:T(8,128)S(1)}, f32[2,130,1]{2,1,0:T(8,128)S(1)}, u32[]{:S(2)}, u32[]{:S(2)}) collective-permute-start(f32[2,130,1]{2,1,0:T(8,128)S(1)} %get-tuple-element.85), channel_id=1, source_target_pairs={{0,1},{1,2},{2,3},{3,4},{4,5},{5,6},{6,7},{7,8},{8,9},{9,10},{10,1... | collective-permute-start | bytes 3128 | tf_op jit(solution)/shard_map/while/body/eval_jaxpr/ppermute | solution.py:16
  172.5 5.0 collective-permute-start
  178.1 7.3 %collective-permute-start.3 = (f32[2,130,1]{2,1,0:T(8,128)S(1)}, f32[2,130,1]{2,1,0:T(8,128)S(1)}, u32[]{:S(2)}, u32[]{:S(2)}) collective-permute-start(f32[2,130,1]{2,1,0:T(8,128)S(1)} %get-tuple-element.85), channel_id=1, source_target_pairs={{0,1},{1,2},{2,3},{3,4},{4,5},{5,6},{6,7},{7,8},{8,9},{9,10},{10,1... | collective-permute-start | bytes 3128 | tf_op jit(solution)/shard_map/while/body/eval_jaxpr/ppermute | solution.py:16
  187.2 5.0 collective-permute-start
  192.8 7.3 %collective-permute-start.3 = (f32[2,130,1]{2,1,0:T(8,128)S(1)}, f32[2,130,1]{2,1,0:T(8,128)S(1)}, u32[]{:S(2)}, u32[]{:S(2)}) collective-permute-start(f32[2,130,1]{2,1,0:T(8,128)S(1)} %get-tuple-element.85), channel_id=1, source_target_pairs={{0,1},{1,2},{2,3},{3,4},{4,5},{5,6},{6,7},{7,8},{8,9},{9,10},{10,1... | collective-permute-start | bytes 3128 | tf_op jit(solution)/shard_map/while/body/eval_jaxpr/ppermute | solution.py:16
  201.9 5.0 collective-permute-start
  207.5 7.3 %collective-permute-start.3 = (f32[2,130,1]{2,1,0:T(8,128)S(1)}, f32[2,130,1]{2,1,0:T(8,128)S(1)}, u32[]{:S(2)}, u32[]{:S(2)}) collective-permute-start(f32[2,130,1]{2,1,0:T(8,128)S(1)} %get-tuple-element.85), channel_id=1, source_target_pairs={{0,1},{1,2},{2,3},{3,4},{4,5},{5,6},{6,7},{7,8},{8,9},{9,10},{10,1... | collective-permute-start | bytes 3128 | tf_op jit(solution)/shard_map/while/body/eval_jaxpr/ppermute | solution.py:16
  216.6 5.0 collective-permute-start
  222.2 7.3 %collective-permute-start.3 = (f32[2,130,1]{2,1,0:T(8,128)S(1)}, f32[2,130,1]{2,1,0:T(8,128)S(1)}, u32[]{:S(2)}, u32[]{:S(2)}) collective-permute-start(f32[2,130,1]{2,1,0:T(8,128)S(1)} %get-tuple-element.85), channel_id=1, source_target_pairs={{0,1},{1,2},{2,3},{3,4},{4,5},{5,6},{6,7},{7,8},{8,9},{9,10},{10,1... | collective-permute-start | bytes 3128 | tf_op jit(solution)/shard_map/while/body/eval_jaxpr/ppermute | solution.py:16
  231.2 5.0 collective-permute-start
  236.9 7.3 %collective-permute-start.3 = (f32[2,130,1]{2,1,0:T(8,128)S(1)}, f32[2,130,1]{2,1,0:T(8,128)S(1)}, u32[]{:S(2)}, u32[]{:S(2)}) collective-permute-start(f32[2,130,1]{2,1,0:T(8,128)S(1)} %get-tuple-element.85), channel_id=1, source_target_pairs={{0,1},{1,2},{2,3},{3,4},{4,5},{5,6},{6,7},{7,8},{8,9},{9,10},{10,1... | collective-permute-start | bytes 3128 | tf_op jit(solution)/shard_map/while/body/eval_jaxpr/ppermute | solution.py:16
  245.9 5.0 collective-permute-start
  251.5 7.3 %collective-permute-start.3 = (f32[2,130,1]{2,1,0:T(8,128)S(1)}, f32[2,130,1]{2,1,0:T(8,128)S(1)}, u32[]{:S(2)}, u32[]{:S(2)}) collective-permute-start(f32[2,130,1]{2,1,0:T(8,128)S(1)} %get-tuple-element.85), channel_id=1, source_target_pairs={{0,1},{1,2},{2,3},{3,4},{4,5},{5,6},{6,7},{7,8},{8,9},{9,10},{10,1... | collective-permute-start | bytes 3128 | tf_op jit(solution)/shard_map/while/body/eval_jaxpr/ppermute | solution.py:16
  260.6 5.0 collective-permute-start
  266.2 7.3 %collective-permute-start.3 = (f32[2,130,1]{2,1,0:T(8,128)S(1)}, f32[2,130,1]{2,1,0:T(8,128)S(1)}, u32[]{:S(2)}, u32[]{:S(2)}) collective-permute-start(f32[2,130,1]{2,1,0:T(8,128)S(1)} %get-tuple-element.85), channel_id=1, source_target_pairs={{0,1},{1,2},{2,3},{3,4},{4,5},{5,6},{6,7},{7,8},{8,9},{9,10},{10,1... | collective-permute-start | bytes 3128 | tf_op jit(solution)/shard_map/while/body/eval_jaxpr/ppermute | solution.py:16
  275.3 5.0 collective-permute-start
  280.9 7.3 %collective-permute-start.3 = (f32[2,130,1]{2,1,0:T(8,128)S(1)}, f32[2,130,1]{2,1,0:T(8,128)S(1)}, u32[]{:S(2)}, u32[]{:S(2)}) collective-permute-start(f32[2,130,1]{2,1,0:T(8,128)S(1)} %get-tuple-element.85), channel_id=1, source_target_pairs={{0,1},{1,2},{2,3},{3,4},{4,5},{5,6},{6,7},{7,8},{8,9},{9,10},{10,1... | collective-permute-start | bytes 3128 | tf_op jit(solution)/shard_map/while/body/eval_jaxpr/ppermute | solution.py:16
  290.0 5.0 collective-permute-start
  295.6 7.3 %collective-permute-start.3 = (f32[2,130,1]{2,1,0:T(8,128)S(1)}, f32[2,130,1]{2,1,0:T(8,128)S(1)}, u32[]{:S(2)}, u32[]{:S(2)}) collective-permute-start(f32[2,130,1]{2,1,0:T(8,128)S(1)} %get-tuple-element.85), channel_id=1, source_target_pairs={{0,1},{1,2},{2,3},{3,4},{4,5},{5,6},{6,7},{7,8},{8,9},{9,10},{10,1... | collective-permute-start | bytes 3128 | tf_op jit(solution)/shard_map/while/body/eval_jaxpr/ppermute | solution.py:16
  304.7 5.0 collective-permute-start
  310.3 7.3 %collective-permute-start.3 = (f32[2,130,1]{2,1,0:T(8,128)S(1)}, f32[2,130,1]{2,1,0:T(8,128)S(1)}, u32[]{:S(2)}, u32[]{:S(2)}) collective-permute-start(f32[2,130,1]{2,1,0:T(8,128)S(1)} %get-tuple-element.85), channel_id=1, source_target_pairs={{0,1},{1,2},{2,3},{3,4},{4,5},{5,6},{6,7},{7,8},{8,9},{9,10},{10,1... | collective-permute-start | bytes 3128 | tf_op jit(solution)/shard_map/while/body/eval_jaxpr/ppermute | solution.py:16
  319.3 5.0 collective-permute-start
  324.9 7.3 %collective-permute-start.3 = (f32[2,130,1]{2,1,0:T(8,128)S(1)}, f32[2,130,1]{2,1,0:T(8,128)S(1)}, u32[]{:S(2)}, u32[]{:S(2)}) collective-permute-start(f32[2,130,1]{2,1,0:T(8,128)S(1)} %get-tuple-element.85), channel_id=1, source_target_pairs={{0,1},{1,2},{2,3},{3,4},{4,5},{5,6},{6,7},{7,8},{8,9},{9,10},{10,1... | collective-permute-start | bytes 3128 | tf_op jit(solution)/shard_map/while/body/eval_jaxpr/ppermute | solution.py:16
  334.0 5.0 collective-permute-start
  339.6 7.3 %collective-permute-start.3 = (f32[2,130,1]{2,1,0:T(8,128)S(1)}, f32[2,130,1]{2,1,0:T(8,128)S(1)}, u32[]{:S(2)}, u32[]{:S(2)}) collective-permute-start(f32[2,130,1]{2,1,0:T(8,128)S(1)} %get-tuple-element.85), channel_id=1, source_target_pairs={{0,1},{1,2},{2,3},{3,4},{4,5},{5,6},{6,7},{7,8},{8,9},{9,10},{10,1... | collective-permute-start | bytes 3128 | tf_op jit(solution)/shard_map/while/body/eval_jaxpr/ppermute | solution.py:16
  348.7 5.0 collective-permute-start
  354.3 7.3 %collective-permute-start.3 = (f32[2,130,1]{2,1,0:T(8,128)S(1)}, f32[2,130,1]{2,1,0:T(8,128)S(1)}, u32[]{:S(2)}, u32[]{:S(2)}) collective-permute-start(f32[2,130,1]{2,1,0:T(8,128)S(1)} %get-tuple-element.85), channel_id=1, source_target_pairs={{0,1},{1,2},{2,3},{3,4},{4,5},{5,6},{6,7},{7,8},{8,9},{9,10},{10,1... | collective-permute-start | bytes 3128 | tf_op jit(solution)/shard_map/while/body/eval_jaxpr/ppermute | solution.py:16
  363.4 5.0 collective-permute-start
  369.0 7.3 %collective-permute-start.3 = (f32[2,130,1]{2,1,0:T(8,128)S(1)}, f32[2,130,1]{2,1,0:T(8,128)S(1)}, u32[]{:S(2)}, u32[]{:S(2)}) collective-permute-start(f32[2,130,1]{2,1,0:T(8,128)S(1)} %get-tuple-element.85), channel_id=1, source_target_pairs={{0,1},{1,2},{2,3},{3,4},{4,5},{5,6},{6,7},{7,8},{8,9},{9,10},{10,1... | collective-permute-start | bytes 3128 | tf_op jit(solution)/shard_map/while/body/eval_jaxpr/ppermute | solution.py:16
  378.1 5.0 collective-permute-start
  383.7 7.3 %collective-permute-start.3 = (f32[2,130,1]{2,1,0:T(8,128)S(1)}, f32[2,130,1]{2,1,0:T(8,128)S(1)}, u32[]{:S(2)}, u32[]{:S(2)}) collective-permute-start(f32[2,130,1]{2,1,0:T(8,128)S(1)} %get-tuple-element.85), channel_id=1, source_target_pairs={{0,1},{1,2},{2,3},{3,4},{4,5},{5,6},{6,7},{7,8},{8,9},{9,10},{10,1... | collective-permute-start | bytes 3128 | tf_op jit(solution)/shard_map/while/body/eval_jaxpr/ppermute | solution.py:16
  392.7 5.0 collective-permute-start
  398.4 7.3 %collective-permute-start.3 = (f32[2,130,1]{2,1,0:T(8,128)S(1)}, f32[2,130,1]{2,1,0:T(8,128)S(1)}, u32[]{:S(2)}, u32[]{:S(2)}) collective-permute-start(f32[2,130,1]{2,1,0:T(8,128)S(1)} %get-tuple-element.85), channel_id=1, source_target_pairs={{0,1},{1,2},{2,3},{3,4},{4,5},{5,6},{6,7},{7,8},{8,9},{9,10},{10,1... | collective-permute-start | bytes 3128 | tf_op jit(solution)/shard_map/while/body/eval_jaxpr/ppermute | solution.py:16
  407.4 5.0 collective-permute-start
  413.0 7.3 %collective-permute-start.3 = (f32[2,130,1]{2,1,0:T(8,128)S(1)}, f32[2,130,1]{2,1,0:T(8,128)S(1)}, u32[]{:S(2)}, u32[]{:S(2)}) collective-permute-start(f32[2,130,1]{2,1,0:T(8,128)S(1)} %get-tuple-element.85), channel_id=1, source_target_pairs={{0,1},{1,2},{2,3},{3,4},{4,5},{5,6},{6,7},{7,8},{8,9},{9,10},{10,1... | collective-permute-start | bytes 3128 | tf_op jit(solution)/shard_map/while/body/eval_jaxpr/ppermute | solution.py:16
  422.1 5.0 collective-permute-start
  427.7 7.3 %collective-permute-start.3 = (f32[2,130,1]{2,1,0:T(8,128)S(1)}, f32[2,130,1]{2,1,0:T(8,128)S(1)}, u32[]{:S(2)}, u32[]{:S(2)}) collective-permute-start(f32[2,130,1]{2,1,0:T(8,128)S(1)} %get-tuple-element.85), channel_id=1, source_target_pairs={{0,1},{1,2},{2,3},{3,4},{4,5},{5,6},{6,7},{7,8},{8,9},{9,10},{10,1... | collective-permute-start | bytes 3128 | tf_op jit(solution)/shard_map/while/body/eval_jaxpr/ppermute | solution.py:16
  436.8 5.0 collective-permute-start
  442.4 7.3 %collective-permute-start.3 = (f32[2,130,1]{2,1,0:T(8,128)S(1)}, f32[2,130,1]{2,1,0:T(8,128)S(1)}, u32[]{:S(2)}, u32[]{:S(2)}) collective-permute-start(f32[2,130,1]{2,1,0:T(8,128)S(1)} %get-tuple-element.85), channel_id=1, source_target_pairs={{0,1},{1,2},{2,3},{3,4},{4,5},{5,6},{6,7},{7,8},{8,9},{9,10},{10,1... | collective-permute-start | bytes 3128 | tf_op jit(solution)/shard_map/while/body/eval_jaxpr/ppermute | solution.py:16
  451.5 5.0 collective-permute-start
  457.1 7.3 %collective-permute-start.3 = (f32[2,130,1]{2,1,0:T(8,128)S(1)}, f32[2,130,1]{2,1,0:T(8,128)S(1)}, u32[]{:S(2)}, u32[]{:S(2)}) collective-permute-start(f32[2,130,1]{2,1,0:T(8,128)S(1)} %get-tuple-element.85), channel_id=1, source_target_pairs={{0,1},{1,2},{2,3},{3,4},{4,5},{5,6},{6,7},{7,8},{8,9},{9,10},{10,1... | collective-permute-start | bytes 3128 | tf_op jit(solution)/shard_map/while/body/eval_jaxpr/ppermute | solution.py:16
  466.2 5.0 collective-permute-start
  471.8 7.3 %collective-permute-start.3 = (f32[2,130,1]{2,1,0:T(8,128)S(1)}, f32[2,130,1]{2,1,0:T(8,128)S(1)}, u32[]{:S(2)}, u32[]{:S(2)}) collective-permute-start(f32[2,130,1]{2,1,0:T(8,128)S(1)} %get-tuple-element.85), channel_id=1, source_target_pairs={{0,1},{1,2},{2,3},{3,4},{4,5},{5,6},{6,7},{7,8},{8,9},{9,10},{10,1... | collective-permute-start | bytes 3128 | tf_op jit(solution)/shard_map/while/body/eval_jaxpr/ppermute | solution.py:16
  (65 other events, 169.1 us)
where the time goes:
time: 609 us; the launch traced here: 608 us
  starting transfers between devices  191 us (31%)
  waiting for transfers between devices  182 us (30%)
  other arithmetic  78.1 us (13%)
  blocking collectives  74.7 us (12%)
  local copies, waits for them, and re-layouts  32.7 us (5%)
  matrix products  24 us (4%)
  loops' own time  23.4 us (4%)
    ppermute x64, starting transfers between devices, padded_2(): lax.ppermute(lax.slice_in_dim(block, 0, width, axis=dim), axis, backward)  146 us
    ppermute x64, waiting for transfers between devices, padded_2(): lax.ppermute(lax.slice_in_dim(block, block.shape[dim] - width, None, axis...  122 us
    psum x1, blocking collectives, local(): gram = lax.psum(local_gram, ('gy', 'gx'))  74.7 us
    ppermute x64, waiting for transfers between devices, padded_2(): lax.ppermute(lax.slice_in_dim(block, 0, width, axis=dim), axis, backward)  60.3 us
    ppermute x64, starting transfers between devices, padded_2(): lax.ppermute(lax.slice_in_dim(block, block.shape[dim] - width, None, axis...  45.1 us
    dynamic_update_slice x32, other arithmetic, local(): final, snaps = lax.scan(one_step, state, rates)  24.1 us
    add x32, other arithmetic, advance(): u_new = u_now + 0.2 * laplace[0] - react + rate * (1.0 - u_now)  23.9 us
    another operation x1, loops' own time, local(): final, snaps = lax.scan(one_step, state, rates)  23.4 us
  transfers between devices with their start and end apart: 128, of which 128 were waited for; matrix products, arithmetic and copies ran while one was open for 3% of the time, Pallas kernels for 0%

commit v1 on v0

v1 whole, which is shorter than its diff:
```python
import functools

import jax
import jax.numpy as jnp
from jax import lax
from jax.experimental import pallas as pl
from jax.experimental.pallas import tpu as pltpu
from jax.sharding import PartitionSpec as P

SNAPS = 32
ROWS = 128
COLS = 256
HALO = 32
PAD = 8
TOP = PAD + HALO
EXT = ROWS + 2 * TOP
BOTTOM = TOP + ROWS
LANES = 128
NGY = 8
NX = 4
NZ = 8
PLANE = NGY * NX
TILES = 2 * ROWS // 8
F32 = jnp.float32
BF16 = jnp.bfloat16
MESH = pl.DeviceIdType.MESH
HIGHEST = lax.Precision.HIGHEST


def iota(shape, dim):
    return lax.broadcasted_iota(jnp.int32, shape, dim)


def lane_roll(value, shift):
    return pltpu.roll(value, shift % LANES, 1)


def pack_first(u, v):
    half = u.shape[0] // 2
    quarter = iota((half, LANES), 1) // HALO
    out = jnp.where(quarter == 0, u[:half], lane_roll(v[:half], HALO))
    out = jnp.where(quarter == 2, lane_roll(u[half:], 2 * HALO), out)
    return jnp.where(quarter == 3, lane_roll(v[half:], 3 * HALO), out)


def pack_last(u, v):
    half = u.shape[0] // 2
    quarter = iota((half, LANES), 1) // HALO
    out = jnp.where(quarter == 3, u[:half], lane_roll(v[:half], -HALO))
    out = jnp.where(quarter == 1, lane_roll(u[half:], -2 * HALO), out)
    return jnp.where(quarter == 0, lane_roll(v[half:], -3 * HALO), out)


def unpack(right, left):
    low = iota(right.shape, 1) < LANES // 2
    u = jnp.concatenate(
        [jnp.where(low, right, left), jnp.where(low, lane_roll(right, -2 * HALO), lane_roll(left, 2 * HALO))], axis=0
    )
    v = jnp.concatenate(
        [
            jnp.where(low, lane_roll(right, -HALO), lane_roll(left, HALO)),
            jnp.where(low, lane_roll(right, -3 * HALO), lane_roll(left, 3 * HALO)),
        ],
        axis=0,
    )
    return u, v


def stencil(state, now, rate, base, rows):
    lane = iota((rows, LANES), 1)
    first = lane == 0
    last = lane == LANES - 1
    centers = []
    sums = []
    for species in range(2):
        mid = [state[now, species, tile, pl.ds(base, rows), :] for tile in range(3)]
        east = [lane_roll(value, -1) for value in mid]
        west = [lane_roll(value, 1) for value in mid]
        total = []
        for tile in range(3):
            north = state[now, species, tile, pl.ds(base - 1, rows), :]
            south = state[now, species, tile, pl.ds(base + 1, rows), :]
            right = jnp.where(last, east[(tile + 1) % 3], east[tile])
            left = jnp.where(first, west[(tile + 2) % 3], west[tile])
            total.append((north + south) + (right + left))
        centers.append(mid)
        sums.append(total)
    keep_u = 0.2 - rate
    keep_v = 0.54 - rate
    for tile in range(3):
        u = centers[0][tile]
        v = centers[1][tile]
        react = u * v * v
        state[now + 1, 0, tile, pl.ds(base, rows), :] = keep_u * u + 0.2 * sums[0][tile] + (rate - react)
        state[now + 1, 1, tile, pl.ds(base, rows), :] = keep_v * v + 0.1 * sums[1][tile] + react


def simulate_kernel(
    ramp, mask_hbm, noise_hbm, cent, gram_out,
    noise, mask, state, side_out, side_in, corner_out, corner_in, gram8, planes, lines,
    in_sem, halo_send, halo_recv, plane_send, plane_recv, line_send, line_recv,
):
    gy = lax.axis_index("gy")
    gx = lax.axis_index("gx")
    z = gx // NX
    x = gx % NX
    up = (gy + NGY - 1) % NGY
    down = (gy + 1) % NGY
    west = (gx + NX * NZ - 1) % (NX * NZ)
    east = (gx + 1) % (NX * NZ)
    me = gy * NX + x

    loads = [
        pltpu.make_async_copy(noise_hbm, noise, in_sem.at[0]),
        pltpu.make_async_copy(mask_hbm, mask, in_sem.at[1]),
    ]
    for load in loads:
        load.start()

    barrier = pltpu.get_barrier_semaphore()
    around = [(up, gx), (down, gx), (gy, west), (gy, east), (up, west), (up, east), (down, west), (down, east)]
    for device in around:
        pl.semaphore_signal(barrier, inc=1, device_id=device, device_id_type=MESH)

    def plane_peer(step):
        peer = (me + step) % PLANE
        return (peer // NX, z * NX + peer % NX)

    def line_peer(step):
        return (gy, ((z + step) % NZ) * NX + x)

    def greet_plane(step, carry):
        pl.semaphore_signal(barrier, inc=1, device_id=plane_peer(step), device_id_type=MESH)
        return carry

    def greet_line(step, carry):
        pl.semaphore_signal(barrier, inc=1, device_id=line_peer(step), device_id_type=MESH)
        return carry

    lax.fori_loop(1, PLANE, greet_plane, 0)
    lax.fori_loop(1, NZ, greet_line, 0)

    for load in loads:
        load.wait()
    row_pos = (gy * ROWS + iota((ROWS, LANES), 0)).astype(F32)
    amplitude = 0.1 * (0.5 + 1.5 * (row_pos + 0.5) / float(ROWS * NGY))
    for tile in range(2):
        lanes = pl.ds(tile * LANES, LANES)
        seeded = mask[:, lanes].astype(F32)
        state[0, 0, tile, pl.ds(TOP, ROWS), :] = 1.0 - 0.5 * seeded + amplitude * noise[0, :, lanes]
        state[0, 1, tile, pl.ds(TOP, ROWS), :] = 0.25 * seeded + amplitude * noise[1, :, lanes]
    inner = pl.ds(TOP, ROWS)
    high_rows = pl.ds(TOP, HALO)
    low_rows = pl.ds(BOTTOM - HALO, HALO)
    side_out[0] = pack_first(state[0, 0, 0, inner, :], state[0, 1, 0, inner, :])
    side_out[1] = pack_last(state[0, 0, 1, inner, :], state[0, 1, 1, inner, :])
    corner_out[0] = pack_first(state[0, 0, 0, high_rows, :], state[0, 1, 0, high_rows, :])
    corner_out[1] = pack_last(state[0, 0, 1, high_rows, :], state[0, 1, 1, high_rows, :])
    corner_out[2] = pack_first(state[0, 0, 0, low_rows, :], state[0, 1, 0, low_rows, :])
    corner_out[3] = pack_last(state[0, 0, 1, low_rows, :], state[0, 1, 1, low_rows, :])

    pl.semaphore_wait(barrier, len(around) + PLANE - 1 + NZ - 1)

    moves = [
        (corner_out.at[0], corner_in.at[2], (up, west)),
        (corner_out.at[1], corner_in.at[3], (up, east)),
        (corner_out.at[2], corner_in.at[0], (down, west)),
        (corner_out.at[3], corner_in.at[1], (down, east)),
        (side_out.at[0], side_in.at[0], (gy, west)),
        (side_out.at[1], side_in.at[1], (gy, east)),
        (
            state.at[0, :, pl.ds(0, 2), high_rows, :],
            state.at[0, :, pl.ds(0, 2), pl.ds(BOTTOM, HALO), :],
            (up, gx),
        ),
        (
            state.at[0, :, pl.ds(0, 2), low_rows, :],
            state.at[0, :, pl.ds(0, 2), pl.ds(PAD, HALO), :],
            (down, gx),
        ),
    ]
    copies = [
        pltpu.make_async_remote_copy(
            src_ref=source, dst_ref=target, send_sem=halo_send.at[i], recv_sem=halo_recv.at[i],
            device_id=device, device_id_type=MESH,
        )
        for i, (source, target, device) in enumerate(moves)
    ]
    for copy in copies:
        copy.start()
    for copy in copies:
        copy.wait()

    for start, right, left in (
        (PAD, corner_in[0], corner_in[1]),
        (TOP, side_in[0], side_in[1]),
        (BOTTOM, corner_in[2], corner_in[3]),
    ):
        u, v = unpack(right, left)
        state[0, 0, 2, pl.ds(start, u.shape[0]), :] = u
        state[0, 1, 2, pl.ds(start, u.shape[0]), :] = v

    for segment in range(5):
        first_step = max(8 * segment - 1, 0)
        end_step = min(8 * segment + 7, SNAPS)
        first_group = 1 + segment
        pairs = 12 - segment

        def one_step(now, carry, first_group=first_group, pairs=pairs):
            rate = 0.01 + 0.008 * ramp[now].astype(F32)

            def one_pair(pair, carry):
                base = pl.multiple_of(8 * first_group + 16 * pair, 8)
                stencil(state, now, rate, base, 16)
                return carry

            return lax.fori_loop(0, pairs, one_pair, carry)

        lax.fori_loop(first_step, end_step, one_step, 0)

    gram8[...] = jnp.zeros_like(gram8)

    def center(group, carry):
        blocks = []
        for species in range(2):
            halves = []
            for tile in range(2):
                snaps = state[pl.ds(1, SNAPS), species, tile, pl.ds(pl.multiple_of(TOP + 8 * group, 8), 8), :]
                average = jnp.sum(snaps, axis=0) * (1.0 / SNAPS)
                halves.append((snaps - average[None]).reshape(8 * SNAPS, LANES))
            block = jnp.concatenate(halves, axis=1).astype(BF16)
            cent[species * (ROWS // 8) + group] = block
            blocks.append(block)
        both = jnp.concatenate(blocks, axis=1)
        gram8[...] += lax.dot_general(both, both, (((1,), (1,)), ((), ())), preferred_element_type=F32)
        return carry

    lax.fori_loop(0, ROWS // 8, center, 0)

    size = 8 * SNAPS
    same = iota((size, size), 0) % 8 == iota((size, size), 1) % 8
    gather_rows = (iota((SNAPS, size), 0) == iota((SNAPS, size), 1) // 8).astype(F32)
    gather_cols = (iota((size, LANES), 0) // 8 == iota((size, LANES), 1) % SNAPS).astype(F32)
    partial = jnp.dot(gather_rows, jnp.where(same, gram8[...], 0.0), precision=HIGHEST, preferred_element_type=F32)
    partial = jnp.dot(partial, gather_cols, precision=HIGHEST, preferred_element_type=F32)
    quarter = iota((8, LANES), 1) // SNAPS
    packed = partial[0:8]
    for part in range(1, 4):
        packed = jnp.where(quarter == part, partial[8 * part : 8 * part + 8], packed)

    planes[me] = packed

    def plane_copy(step):
        return pltpu.make_async_remote_copy(
            src_ref=planes.at[me], dst_ref=planes.at[me], send_sem=plane_send, recv_sem=plane_recv,
            device_id=plane_peer(step), device_id_type=MESH,
        )

    def send_plane(step, carry):
        plane_copy(step).start()
        return carry

    lax.fori_loop(1, PLANE, send_plane, 0)
    whole = pltpu.make_async_remote_copy(
        src_ref=planes.at[pl.ds(0, PLANE - 1)], dst_ref=planes.at[pl.ds(0, PLANE - 1)],
        send_sem=plane_send, recv_sem=plane_recv, device_id=plane_peer(1), device_id_type=MESH,
    )
    whole.wait()
    lines[z] = jnp.sum(planes[...], axis=0)

    def send_line(step, carry):
        pltpu.make_async_remote_copy(
            src_ref=lines.at[z], dst_ref=lines.at[z], send_sem=line_send, recv_sem=line_recv,
            device_id=line_peer(step), device_id_type=MESH,
        ).start()
        return carry

    lax.fori_loop(1, NZ, send_line, 0)
    whole = pltpu.make_async_remote_copy(
        src_ref=lines.at[pl.ds(0, NZ - 1)], dst_ref=lines.at[pl.ds(0, NZ - 1)],
        send_sem=line_send, recv_sem=line_recv, device_id=line_peer(1), device_id_type=MESH,
    )
    whole.wait()
    gram_out[...] = jnp.sum(lines[...], axis=0)


def simulate(ramp, seed_mask, noise):
    size = 8 * SNAPS
    return pl.pallas_call(
        simulate_kernel,
        name="simulate",
        out_shape=(
            pltpu.VMEM((TILES, size, COLS), BF16),
            jax.ShapeDtypeStruct((8, LANES), F32),
        ),
        in_specs=[
            pl.BlockSpec(memory_space=pltpu.SMEM),
            pl.BlockSpec(memory_space=pl.ANY),
            pl.BlockSpec(memory_space=pl.ANY),
        ],
        out_specs=(pl.BlockSpec(memory_space=pltpu.VMEM), pl.BlockSpec(memory_space=pltpu.VMEM)),
        scratch_shapes=[
            pltpu.VMEM((2, ROWS, COLS), F32),
            pltpu.VMEM((ROWS, COLS), jnp.int32),
            pltpu.VMEM((SNAPS + 1, 2, 3, EXT, LANES), F32),
            pltpu.VMEM((2, ROWS // 2, LANES), F32),
            pltpu.VMEM((2, ROWS // 2, LANES), F32),
            pltpu.VMEM((4, HALO // 2, LANES), F32),
            pltpu.VMEM((4, HALO // 2, LANES), F32),
            pltpu.VMEM((size, size), F32),
            pltpu.VMEM((PLANE, 8, LANES), F32),
            pltpu.VMEM((NZ, 8, LANES), F32),
            pltpu.SemaphoreType.DMA((2,)),
            pltpu.SemaphoreType.DMA((8,)),
            pltpu.SemaphoreType.DMA((8,)),
            pltpu.SemaphoreType.DMA,
            pltpu.SemaphoreType.DMA,
            pltpu.SemaphoreType.DMA,
            pltpu.SemaphoreType.DMA,
        ],
        compiler_params=pltpu.CompilerParams(
            collective_id=0, has_side_effects=True, vmem_limit_bytes=40 * 1024 * 1024
        ),
    )(ramp, seed_mask, noise)


def solve(packed):
    gram = jnp.concatenate([lane_roll(packed, -SNAPS * part) for part in range(4)], axis=0)
    row = iota((SNAPS, LANES), 0)
    lane = iota((SNAPS, LANES), 1)
    diagonal = row == lane
    trace = jnp.sum(jnp.where(diagonal, gram, 0.0), axis=(0, 1), keepdims=True)
    shift = 0.01 * trace / SNAPS
    left = gram + jnp.where(diagonal, shift, 0.0)
    work = jnp.where(lane < SNAPS, left, lane_roll(gram, SNAPS))
    for k in range(SNAPS):
        pivot_row = work[k : k + 1, :]
        scaled = pivot_row / work[k : k + 1, k : k + 1]
        work = jnp.where(row == k, scaled, work - work[:, k : k + 1] * scaled)
    return lane_roll(work, -SNAPS)


def filter_kernel(cent, packed, out, matrix_out, weights):
    @pl.when(pl.program_id(0) == 0)
    def _():
        matrix = solve(packed[...])
        matrix_out[...] = matrix[:, :SNAPS]
        size = 8 * SNAPS
        spread_rows = (iota((size, SNAPS), 0) // 8 == iota((size, SNAPS), 1)).astype(BF16)
        spread_cols = (iota((SNAPS, size), 0) == iota((SNAPS, size), 1) // 8).astype(BF16)
        turned = jnp.transpose(matrix)[:SNAPS, :].astype(BF16)
        wide = jnp.dot(spread_rows, turned, preferred_element_type=F32).astype(BF16)
        wide = jnp.dot(wide, spread_cols, preferred_element_type=F32)
        same = iota((size, size), 0) % 8 == iota((size, size), 1) % 8
        weights[...] = jnp.where(same, wide, 0.0).astype(BF16)

    for part in range(cent.shape[0]):
        block = jnp.dot(weights[...], cent[part], preferred_element_type=F32)
        out[:, 0, pl.ds(8 * part, 8), :] = block.reshape(SNAPS, 8, COLS)


def apply_filter(cent, packed):
    size = 8 * SNAPS
    parts = 2
    steps = TILES // parts
    per_species = steps // 2
    return pl.pallas_call(
        filter_kernel,
        name="apply_filter",
        grid=(steps,),
        out_shape=(
            jax.ShapeDtypeStruct((SNAPS, 2, ROWS, COLS), F32),
            jax.ShapeDtypeStruct((SNAPS, SNAPS), F32),
        ),
        in_specs=[
            pl.BlockSpec((parts, size, COLS), lambda i: (i, 0, 0)),
            pl.BlockSpec((8, LANES), lambda i: (0, 0)),
        ],
        out_specs=(
            pl.BlockSpec((SNAPS, 1, 8 * parts, COLS), lambda i: (0, i // per_species, i % per_species, 0)),
            pl.BlockSpec((SNAPS, SNAPS), lambda i: (0, 0)),
        ),
        scratch_shapes=[pltpu.VMEM((size, size), BF16)],
        compiler_params=pltpu.CompilerParams(vmem_limit_bytes=16 * 1024 * 1024),
    )(cent, packed)


def local(ramp, seed_mask, noise):
    cent, packed = simulate(ramp, seed_mask, noise)
    return apply_filter(cent, packed)


def solution(mesh):
    return jax.shard_map(
        local,
        mesh=mesh,
        in_specs=(P(), P("gy", "gx"), P(None, "gy", "gx")),
        out_specs=(P(None, None, "gy", "gx"), P()),
        check_vma=False,
    )
```

time: 609 us -> 79.6 us (0.13)
  starting transfers between devices: 191 us -> 0 us
  waiting for transfers between devices: 182 us -> 0 us
  other arithmetic: 78.1 us -> 0 us
  Pallas kernels: 0 us -> 76.3 us
  blocking collectives: 74.7 us -> 0 us
  local copies, waits for them, and re-layouts: 32.7 us -> 2.5 us
  matrix products: 24 us -> 0 us
  loops' own time: 23.4 us -> 0 us
    ppermute x128 -> x0, starting transfers between devices: 191 us -> none  [the longest x64 146 us: padded_2(): lax.ppermute(lax.slice_in_dim(block, 0, width, axis=dim), axis, backward)]
    ppermute x128 -> x0, waiting for transfers between devices: 182 us -> none  [the longest x64 122 us: padded_2(): lax.ppermute(lax.slice_in_dim(block, block.shape[dim] - width, None, axis...]
    pallas_call x0 -> x2, Pallas kernels: none -> 76.3 us  [the longest x1 64.5 us: simulate(): pl.pallas_call(simulate_kernel, name='simulate', out_shape=(pltpu.VMEM((T...]
    psum x1 -> x0, blocking collectives: 74.7 us -> none  [local(): gram = lax.psum(local_gram, ('gy', 'gx'))]
    dynamic_update_slice x32 -> x0, other arithmetic: 24.1 us -> none  [local(): final, snaps = lax.scan(one_step, state, rates)]
    add x34 -> x0, other arithmetic: 24 us -> none  [the longest x32 23.9 us: advance(): u_new = u_now + 0.2 * laplace[0] - react + rate * (1.0 - u_now)]
    dot_general x2 -> x0, matrix products: 23.6 us -> none  [the longest x1 12.7 us: local(): jnp.dot(filter_matrix.T, flat, precision=lax.Precision.HIGHEST, preferred...]
    another operation x1 -> x0, loops' own time: 23.4 us -> none  [local(): final, snaps = lax.scan(one_step, state, rates)]
  transfers between devices with their start and end apart: 128 -> 0, of which waited for: 128 -> 0; matrix products, arithmetic and copies ran while one was open for 3% -> 0% of each run, Pallas kernels for 0% -> 0%
where the time goes in v1:
time: 79.6 us; the launch traced here: 79.4 us
  Pallas kernels  76.3 us (96%)
  local copies, waits for them, and re-layouts  2.5 us (3%)
    pallas_call x1, Pallas kernels, simulate(): pl.pallas_call(simulate_kernel, name='simulate', out_shape=(pltpu.VMEM((T...  64.5 us
    pallas_call x1, Pallas kernels, apply_filter(): pl.pallas_call(filter_kernel, name='apply_filter', grid=(steps,), out_sha...  11.8 us
    unnamed x6, local copies, waits for them, and re-layouts  2.5 us

profile of v1, /device:TPU:1, one launch (start us, length us, event | category | flops | bytes accessed | tf_op | source)
XLA Modules:
  0.0 79.4 jit_solution(8664664569114070529)
XLA Ops:
  0.6 0.0 copy-start
  0.6 0.9 %copy-done = f32[2,128,256]{2,1,0:T(8,128)S(1)} copy-done((f32[2,128,256]{2,1,0:T(8,128)S(1)}, f32[2,128,256]{2,1,0:T(8,128)}, u32[]{:S(2)}) %copy-start) | copy-done | bytes 262168
  1.6 0.0 copy-start.1
  1.6 0.9 %copy-done.1 = s32[128,256]{1,0:T(8,128)S(1)} copy-done((s32[128,256]{1,0:T(8,128)S(1)}, s32[128,256]{1,0:T(8,128)}, u32[]{:S(2)}) %copy-start.1) | copy-done | bytes 131096
  2.5 0.0 copy-start.2
  2.5 0.7 copy-done.2
  3.1 64.5 %simulate.1 = (bf16[32,256,256]{2,1,0:T(8,128)(2,1)S(1)}, f32[8,128]{1,0:T(8,128)S(1)}) custom-call(s32[32]{0:T(128)S(1)} %copy-done.2, s32[128,256]{1,0:T(8,128)S(1)} %copy-done.1, f32[2,128,256]{2,1,0:T(8,128)S(1)} %copy-done), custom_call_target="tpu_custom_call" | custom-call | tf_op jit(solution)/shard_map/simulate/pallas_call | solution.py:289
  67.6 11.8 %apply_filter.1 = (f32[32,2,128,256]{3,2,1,0:T(8,128)}, f32[32,32]{1,0:T(8,128)}) custom-call(bf16[32,256,256]{2,1,0:T(8,128)(2,1)S(1)} %get-tuple-element.4.cent, f32[8,128]{1,0:T(8,128)S(1)} %get-tuple-element.5.packed), custom_call_target="tpu_custom_call" | custom-call | tf_op jit(solution)/shard_map/apply_filter/pallas_call | solution.py:367
Async XLA Ops:
  0.6 1.0 %copy-start = (f32[2,128,256]{2,1,0:T(8,128)S(1)}, f32[2,128,256]{2,1,0:T(8,128)}, u32[]{:S(2)}) copy-start(f32[2,128,256]{2,1,0:T(8,128)} %noise_hbm.1) | copy-start | bytes 786436
  1.6 0.9 %copy-start.1 = (s32[128,256]{1,0:T(8,128)S(1)}, s32[128,256]{1,0:T(8,128)}, u32[]{:S(2)}) copy-start(s32[128,256]{1,0:T(8,128)} %mask_hbm.1) | copy-start | bytes 393220
  2.5 0.7 copy-start.2

commit v2 on v1

--- a/solution.py
+++ b/solution.py
@@ -1,5 +1,3 @@
-import functools
-
 import jax
 import jax.numpy as jnp
 from jax import lax
@@ -16,6 +14,7 @@
 EXT = ROWS + 2 * TOP
 BOTTOM = TOP + ROWS
 LANES = 128
+WIDE = 3 * LANES
 NGY = 8
 NX = 4
 NZ = 8
@@ -24,7 +23,6 @@
 F32 = jnp.float32
 BF16 = jnp.bfloat16
 MESH = pl.DeviceIdType.MESH
-HIGHEST = lax.Precision.HIGHEST
 
 
 def iota(shape, dim):
@@ -66,23 +64,36 @@
     return u, v
 
 
+def woven(index):
+    return 3 * (index % LANES) + index // LANES - LANES // 2
+
+
+def split(value):
+    high = value.astype(BF16)
+    rest = value - high.astype(F32)
+    middle = rest.astype(BF16)
+    low = (rest - middle.astype(F32)).astype(BF16)
+    return [high, middle, low]
+
+
+def select_columns(values, choice):
+    rows = values.shape[0]
+    out = jnp.dot(jnp.concatenate(split(values), axis=0), choice, preferred_element_type=F32)
+    return (out[:rows] + out[rows : 2 * rows]) + out[2 * rows :]
+
+
 def stencil(state, now, rate, base, rows):
-    lane = iota((rows, LANES), 1)
-    first = lane == 0
-    last = lane == LANES - 1
     centers = []
     sums = []
     for species in range(2):
         mid = [state[now, species, tile, pl.ds(base, rows), :] for tile in range(3)]
-        east = [lane_roll(value, -1) for value in mid]
-        west = [lane_roll(value, 1) for value in mid]
+        east = [mid[1], mid[2], lane_roll(mid[0], -1)]
+        west = [lane_roll(mid[2], 1), mid[0], mid[1]]
         total = []
         for tile in range(3):
             north = state[now, species, tile, pl.ds(base - 1, rows), :]
             south = state[now, species, tile, pl.ds(base + 1, rows), :]
-            right = jnp.where(last, east[(tile + 1) % 3], east[tile])
-            left = jnp.where(first, west[(tile + 2) % 3], west[tile])
-            total.append((north + south) + (right + left))
+            total.append((north + south) + (east[tile] + west[tile]))
         centers.append(mid)
         sums.append(total)
     keep_u = 0.2 - rate
@@ -97,7 +108,8 @@
 
 def simulate_kernel(
     ramp, mask_hbm, noise_hbm, cent, gram_out,
-    noise, mask, state, side_out, side_in, corner_out, corner_in, gram8, planes, lines,
+    noise, mask, nat, state, woven_cent, side_out, side_in, corner_out, corner_in, own_choice, side_choice,
+    back_choice, gram8, planes, lines,
     in_sem, halo_send, halo_recv, plane_send, plane_recv, line_send, line_recv,
 ):
     gy = lax.axis_index("gy")
@@ -140,44 +152,50 @@
     lax.fori_loop(1, PLANE, greet_plane, 0)
     lax.fori_loop(1, NZ, greet_line, 0)
 
+    own_choice[...] = (iota((COLS, WIDE), 0) == woven(iota((COLS, WIDE), 1))).astype(BF16)
+    lane = iota((LANES, WIDE), 0)
+    side_column = jnp.where(lane < LANES // 2, COLS + lane, lane - LANES)
+    side_choice[...] = (side_column == woven(iota((LANES, WIDE), 1))).astype(BF16)
+    back_choice[...] = (woven(iota((WIDE, COLS), 0)) == iota((WIDE, COLS), 1)).astype(BF16)
+
     for load in loads:
         load.wait()
     row_pos = (gy * ROWS + iota((ROWS, LANES), 0)).astype(F32)
     amplitude = 0.1 * (0.5 + 1.5 * (row_pos + 0.5) / float(ROWS * NGY))
+    own_rows = pl.ds(HALO, ROWS)
     for tile in range(2):
         lanes = pl.ds(tile * LANES, LANES)
         seeded = mask[:, lanes].astype(F32)
-        state[0, 0, tile, pl.ds(TOP, ROWS), :] = 1.0 - 0.5 * seeded + amplitude * noise[0, :, lanes]
-        state[0, 1, tile, pl.ds(TOP, ROWS), :] = 0.25 * seeded + amplitude * noise[1, :, lanes]
-    inner = pl.ds(TOP, ROWS)
-    high_rows = pl.ds(TOP, HALO)
-    low_rows = pl.ds(BOTTOM - HALO, HALO)
-    side_out[0] = pack_first(state[0, 0, 0, inner, :], state[0, 1, 0, inner, :])
-    side_out[1] = pack_last(state[0, 0, 1, inner, :], state[0, 1, 1, inner, :])
-    corner_out[0] = pack_first(state[0, 0, 0, high_rows, :], state[0, 1, 0, high_rows, :])
-    corner_out[1] = pack_last(state[0, 0, 1, high_rows, :], state[0, 1, 1, high_rows, :])
-    corner_out[2] = pack_first(state[0, 0, 0, low_rows, :], state[0, 1, 0, low_rows, :])
-    corner_out[3] = pack_last(state[0, 0, 1, low_rows, :], state[0, 1, 1, low_rows, :])
+        nat[0, tile, own_rows, :] = 1.0 - 0.5 * seeded + amplitude * noise[0, :, lanes]
+        nat[1, tile, own_rows, :] = 0.25 * seeded + amplitude * noise[1, :, lanes]
+    high_rows = pl.ds(HALO, HALO)
+    low_rows = pl.ds(ROWS, HALO)
+    side_out[0] = pack_first(nat[0, 0, own_rows, :], nat[1, 0, own_rows, :])
+    side_out[1] = pack_last(nat[0, 1, own_rows, :], nat[1, 1, own_rows, :])
+    corner_out[0] = pack_first(nat[0, 0, high_rows, :], nat[1, 0, high_rows, :])
+    corner_out[1] = pack_last(nat[0, 1, high_rows, :], nat[1, 1, high_rows, :])
+    corner_out[2] = pack_first(nat[0, 0, low_rows, :], nat[1, 0, low_rows, :])
+    corner_out[3] = pack_last(nat[0, 1, low_rows, :], nat[1, 1, low_rows, :])
+
+    def natural(species, rows):
+        return jnp.concatenate([nat[species, 0, rows, :], nat[species, 1, rows, :]], axis=1)
+
+    for species in range(2):
+        placed = select_columns(natural(species, own_rows), own_choice[...])
+        for tile in range(3):
+            state[0, species, tile, pl.ds(TOP, ROWS), :] = placed[:, LANES * tile : LANES * (tile + 1)]
 
     pl.semaphore_wait(barrier, len(around) + PLANE - 1 + NZ - 1)
 
     moves = [
+        (side_out.at[0], side_in.at[0], (gy, west)),
+        (side_out.at[1], side_in.at[1], (gy, east)),
         (corner_out.at[0], corner_in.at[2], (up, west)),
         (corner_out.at[1], corner_in.at[3], (up, east)),
         (corner_out.at[2], corner_in.at[0], (down, west)),
         (corner_out.at[3], corner_in.at[1], (down, east)),
-        (side_out.at[0], side_in.at[0], (gy, west)),
-        (side_out.at[1], side_in.at[1], (gy, east)),
-        (
-            state.at[0, :, pl.ds(0, 2), high_rows, :],
-            state.at[0, :, pl.ds(0, 2), pl.ds(BOTTOM, HALO), :],
-            (up, gx),
-        ),
-        (
-            state.at[0, :, pl.ds(0, 2), low_rows, :],
-            state.at[0, :, pl.ds(0, 2), pl.ds(PAD, HALO), :],
-            (down, gx),
-        ),
+        (nat.at[:, :, high_rows, :], nat.at[:, :, pl.ds(HALO + ROWS, HALO), :], (up, gx)),
+        (nat.at[:, :, low_rows, :], nat.at[:, :, pl.ds(0, HALO), :], (down, gx)),
     ]
     copies = [
         pltpu.make_async_remote_copy(
@@ -191,14 +209,23 @@
     for copy in copies:
         copy.wait()
 
-    for start, right, left in (
-        (PAD, corner_in[0], corner_in[1]),
-        (TOP, side_in[0], side_in[1]),
-        (BOTTOM, corner_in[2], corner_in[3]),
-    ):
-        u, v = unpack(right, left)
-        state[0, 0, 2, pl.ds(start, u.shape[0]), :] = u
-        state[0, 1, 2, pl.ds(start, u.shape[0]), :] = v
+    sides = [
+        unpack(corner_in[0], corner_in[1]),
+        unpack(side_in[0], side_in[1]),
+        unpack(corner_in[2], corner_in[3]),
+    ]
+    for species in range(2):
+        beside = jnp.concatenate([side[species] for side in sides], axis=0)
+        beside = select_columns(beside, side_choice[...])
+        edge = jnp.concatenate(
+            [natural(species, pl.ds(0, HALO)), natural(species, pl.ds(HALO + ROWS, HALO))], axis=0
+        )
+        edge = select_columns(edge, own_choice[...])
+        for tile in range(3):
+            lanes = slice(LANES * tile, LANES * (tile + 1))
+            state[0, species, tile, pl.ds(PAD, HALO), :] = beside[:HALO, lanes] + edge[:HALO, lanes]
+            state[0, species, tile, pl.ds(TOP, ROWS), :] += beside[HALO : HALO + ROWS, lanes]
+            state[0, species, tile, pl.ds(BOTTOM, HALO), :] = beside[HALO + ROWS :, lanes] + edge[HALO:, lanes]
 
     for segment in range(5):
         first_step = max(8 * segment - 1, 0)
@@ -214,35 +241,44 @@
                 stencil(state, now, rate, base, 16)
                 return carry
 
-            return lax.fori_loop(0, pairs, one_pair, carry)
+            return lax.fori_loop(0, pairs, one_pair, carry, unroll=True)
 
         lax.fori_loop(first_step, end_step, one_step, 0)
 
     gram8[...] = jnp.zeros_like(gram8)
-
-    def center(group, carry):
+    groups = 4
+    column = 3 * iota((8, LANES), 1) - LANES // 2
+
+    def center(step, carry):
         blocks = []
-        for species in range(2):
-            halves = []
-            for tile in range(2):
-                snaps = state[pl.ds(1, SNAPS), species, tile, pl.ds(pl.multiple_of(TOP + 8 * group, 8), 8), :]
-                average = jnp.sum(snaps, axis=0) * (1.0 / SNAPS)
-                halves.append((snaps - average[None]).reshape(8 * SNAPS, LANES))
-            block = jnp.concatenate(halves, axis=1).astype(BF16)
-            cent[species * (ROWS // 8) + group] = block
-            blocks.append(block)
+        for group in range(groups):
+            base = pl.multiple_of(TOP + 8 * groups * step + 8 * group, 8)
+            for species in range(2):
+                thirds = []
+                for tile in range(3):
+                    inside = (column + tile >= 0) & (column + tile < COLS)
+                    snaps = state[pl.ds(1, SNAPS), species, tile, pl.ds(base, 8), :]
+                    average = jnp.sum(snaps, axis=0) * (1.0 / SNAPS)
+                    centered = jnp.where(inside[None], snaps - average[None], 0.0)
+                    thirds.append(centered.reshape(8 * SNAPS, LANES).astype(BF16))
+                block = jnp.concatenate(thirds, axis=1)
+                woven_cent[species * (ROWS // 8) + groups * step + group] = block
+                blocks.append(block)
         both = jnp.concatenate(blocks, axis=1)
         gram8[...] += lax.dot_general(both, both, (((1,), (1,)), ((), ())), preferred_element_type=F32)
         return carry
 
-    lax.fori_loop(0, ROWS // 8, center, 0)
+    lax.fori_loop(0, ROWS // (8 * groups), center, 0)
 
     size = 8 * SNAPS
     same = iota((size, size), 0) % 8 == iota((size, size), 1) % 8
-    gather_rows = (iota((SNAPS, size), 0) == iota((SNAPS, size), 1) // 8).astype(F32)
-    gather_cols = (iota((size, LANES), 0) // 8 == iota((size, LANES), 1) % SNAPS).astype(F32)
-    partial = jnp.dot(gather_rows, jnp.where(same, gram8[...], 0.0), precision=HIGHEST, preferred_element_type=F32)
-    partial = jnp.dot(partial, gather_cols, precision=HIGHEST, preferred_element_type=F32)
+    gather_rows = (iota((SNAPS, size), 0) == iota((SNAPS, size), 1) // 8).astype(BF16)
+    gather_cols = (iota((size, LANES), 0) // 8 == iota((size, LANES), 1) % SNAPS).astype(BF16)
+    pieces = [
+        jnp.dot(gather_rows, piece, preferred_element_type=F32) for piece in split(jnp.where(same, gram8[...], 0.0))
+    ]
+    partial = (pieces[0] + pieces[1]) + pieces[2]
+    partial = select_columns(partial, gather_cols)
     quarter = iota((8, LANES), 1) // SNAPS
     packed = partial[0:8]
     for part in range(1, 4):
@@ -250,17 +286,21 @@
 
     planes[me] = packed
 
-    def plane_copy(step):
-        return pltpu.make_async_remote_copy(
+    def send_plane(step, carry):
+        pltpu.make_async_remote_copy(
             src_ref=planes.at[me], dst_ref=planes.at[me], send_sem=plane_send, recv_sem=plane_recv,
             device_id=plane_peer(step), device_id_type=MESH,
-        )
-
-    def send_plane(step, carry):
-        plane_copy(step).start()
+        ).start()
+        return carry
+
+    def unweave(part, carry):
+        for k in range(4):
+            tile = 4 * part + k
+            cent[tile] = jnp.dot(woven_cent[tile], back_choice[...], preferred_element_type=F32).astype(BF16)
         return carry
 
     lax.fori_loop(1, PLANE, send_plane, 0)
+    lax.fori_loop(0, TILES // 8, unweave, 0)
     whole = pltpu.make_async_remote_copy(
         src_ref=planes.at[pl.ds(0, PLANE - 1)], dst_ref=planes.at[pl.ds(0, PLANE - 1)],
         send_sem=plane_send, recv_sem=plane_recv, device_id=plane_peer(1), device_id_type=MESH,
@@ -276,6 +316,7 @@
         return carry
 
     lax.fori_loop(1, NZ, send_line, 0)
+    lax.fori_loop(TILES // 8, TILES // 4, unweave, 0)
     whole = pltpu.make_async_remote_copy(
         src_ref=lines.at[pl.ds(0, NZ - 1)], dst_ref=lines.at[pl.ds(0, NZ - 1)],
         send_sem=line_send, recv_sem=line_recv, device_id=line_peer(1), device_id_type=MESH,
@@ -295,18 +336,23 @@
         ),
         in_specs=[
             pl.BlockSpec(memory_space=pltpu.SMEM),
-            pl.BlockSpec(memory_space=pl.ANY),
-            pl.BlockSpec(memory_space=pl.ANY),
+            pl.BlockSpec(memory_space=pltpu.HBM),
+            pl.BlockSpec(memory_space=pltpu.HBM),
         ],
         out_specs=(pl.BlockSpec(memory_space=pltpu.VMEM), pl.BlockSpec(memory_space=pltpu.VMEM)),
         scratch_shapes=[
             pltpu.VMEM((2, ROWS, COLS), F32),
             pltpu.VMEM((ROWS, COLS), jnp.int32),
+            pltpu.VMEM((2, 2, ROWS + 2 * HALO, LANES), F32),
             pltpu.VMEM((SNAPS + 1, 2, 3, EXT, LANES), F32),
+            pltpu.VMEM((TILES, size, WIDE), BF16),
             pltpu.VMEM((2, ROWS // 2, LANES), F32),
             pltpu.VMEM((2, ROWS // 2, LANES), F32),
             pltpu.VMEM((4, HALO // 2, LANES), F32),
             pltpu.VMEM((4, HALO // 2, LANES), F32),
+            pltpu.VMEM((COLS, WIDE), BF16),
+            pltpu.VMEM((LANES, WIDE), BF16),
+            pltpu.VMEM((WIDE, COLS), BF16),
             pltpu.VMEM((size, size), F32),
             pltpu.VMEM((PLANE, 8, LANES), F32),
             pltpu.VMEM((NZ, 8, LANES), F32),
@@ -319,7 +365,7 @@
             pltpu.SemaphoreType.DMA,
         ],
         compiler_params=pltpu.CompilerParams(
-            collective_id=0, has_side_effects=True, vmem_limit_bytes=40 * 1024 * 1024
+            collective_id=0, has_side_effects=True, vmem_limit_bytes=44 * 1024 * 1024
         ),
     )(ramp, seed_mask, noise)
 
@@ -361,7 +407,7 @@
 
 def apply_filter(cent, packed):
     size = 8 * SNAPS
-    parts = 2
+    parts = 8
     steps = TILES // parts
     per_species = steps // 2
     return pl.pallas_call(
@@ -381,7 +427,7 @@
             pl.BlockSpec((SNAPS, SNAPS), lambda i: (0, 0)),
         ),
         scratch_shapes=[pltpu.VMEM((size, size), BF16)],
-        compiler_params=pltpu.CompilerParams(vmem_limit_bytes=16 * 1024 * 1024),
+        compiler_params=pltpu.CompilerParams(vmem_limit_bytes=12 * 1024 * 1024),
     )(cent, packed)
 
 

time: 79.6 us -> 46.3 us (0.58)
  Pallas kernels: 76.3 us -> 43 us
    pallas_call x1, Pallas kernels: 64.5 us -> 35.4 us  [simulate(): pl.pallas_call(simulate_kernel, name='simulate', out_shape=(pltpu.VMEM((T...]
    pallas_call x1, Pallas kernels: 11.8 us -> 7.55 us  [apply_filter(): pl.pallas_call(filter_kernel, name='apply_filter', grid=(steps,), out_sha...]
where the time goes in v2:
time: 46.3 us; the launch traced here: 46.1 us
  Pallas kernels  43 us (93%)
  local copies, waits for them, and re-layouts  2.5 us (5%)
  between operations  0.65 us (1%)
    pallas_call x1, Pallas kernels, simulate(): pl.pallas_call(simulate_kernel, name='simulate', out_shape=(pltpu.VMEM((T...  35.4 us
    pallas_call x1, Pallas kernels, apply_filter(): pl.pallas_call(filter_kernel, name='apply_filter', grid=(steps,), out_sha...  7.55 us
    unnamed x6, local copies, waits for them, and re-layouts  2.5 us

profile of v2, /device:TPU:1, one launch (start us, length us, event | category | flops | bytes accessed | tf_op | source)
XLA Modules:
  0.0 46.1 jit_solution(12703656799915004858)
XLA Ops:
  0.6 0.0 copy-start
  0.6 0.9 %copy-done = f32[2,128,256]{2,1,0:T(8,128)S(1)} copy-done((f32[2,128,256]{2,1,0:T(8,128)S(1)}, f32[2,128,256]{2,1,0:T(8,128)}, u32[]{:S(2)}) %copy-start) | copy-done | bytes 262168
  1.6 0.0 copy-start.1
  1.6 0.9 %copy-done.1 = s32[128,256]{1,0:T(8,128)S(1)} copy-done((s32[128,256]{1,0:T(8,128)S(1)}, s32[128,256]{1,0:T(8,128)}, u32[]{:S(2)}) %copy-start.1) | copy-done | bytes 131096
  2.5 0.0 copy-start.2
  2.5 0.7 %copy-done.2 = s32[32]{0:T(128)S(1)} copy-done((s32[32]{0:T(128)S(1)}, s32[32]{0:T(128)}, u32[]{:S(2)}) %copy-start.2) | copy-done | bytes 152
  3.1 35.4 %simulate.1 = (bf16[32,256,256]{2,1,0:T(8,128)(2,1)S(1)}, f32[8,128]{1,0:T(8,128)S(1)}) custom-call(s32[32]{0:T(128)S(1)} %copy-done.2, s32[128,256]{1,0:T(8,128)S(1)} %copy-done.1, f32[2,128,256]{2,1,0:T(8,128)S(1)} %copy-done), custom_call_target="tpu_custom_call" | custom-call | tf_op jit(solution)/shard_map/simulate/pallas_call | solution.py:330
  38.6 7.5 %apply_filter.1 = (f32[32,2,128,256]{3,2,1,0:T(8,128)}, f32[32,32]{1,0:T(8,128)}) custom-call(bf16[32,256,256]{2,1,0:T(8,128)(2,1)S(1)} %get-tuple-element.4.cent, f32[8,128]{1,0:T(8,128)S(1)} %get-tuple-element.5.packed), custom_call_target="tpu_custom_call" | custom-call | tf_op jit(solution)/shard_map/apply_filter/pallas_call | solution.py:413
Async XLA Ops:
  0.6 1.0 %copy-start = (f32[2,128,256]{2,1,0:T(8,128)S(1)}, f32[2,128,256]{2,1,0:T(8,128)}, u32[]{:S(2)}) copy-start(f32[2,128,256]{2,1,0:T(8,128)} %noise_hbm.1) | copy-start | bytes 786436
  1.6 0.9 %copy-start.1 = (s32[128,256]{1,0:T(8,128)S(1)}, s32[128,256]{1,0:T(8,128)}, u32[]{:S(2)}) copy-start(s32[128,256]{1,0:T(8,128)} %mask_hbm.1) | copy-start | bytes 393220
  2.5 0.7 %copy-start.2 = (s32[32]{0:T(128)S(1)}, s32[32]{0:T(128)}, u32[]{:S(2)}) copy-start(s32[32]{0:T(128)} %ramp.1) | copy-start | bytes 388

commit v3 on v2

--- a/solution.py
+++ b/solution.py
@@ -152,12 +152,6 @@
     lax.fori_loop(1, PLANE, greet_plane, 0)
     lax.fori_loop(1, NZ, greet_line, 0)
 
-    own_choice[...] = (iota((COLS, WIDE), 0) == woven(iota((COLS, WIDE), 1))).astype(BF16)
-    lane = iota((LANES, WIDE), 0)
-    side_column = jnp.where(lane < LANES // 2, COLS + lane, lane - LANES)
-    side_choice[...] = (side_column == woven(iota((LANES, WIDE), 1))).astype(BF16)
-    back_choice[...] = (woven(iota((WIDE, COLS), 0)) == iota((WIDE, COLS), 1)).astype(BF16)
-
     for load in loads:
         load.wait()
     row_pos = (gy * ROWS + iota((ROWS, LANES), 0)).astype(F32)
@@ -177,14 +171,6 @@
     corner_out[2] = pack_first(nat[0, 0, low_rows, :], nat[1, 0, low_rows, :])
     corner_out[3] = pack_last(nat[0, 1, low_rows, :], nat[1, 1, low_rows, :])
 
-    def natural(species, rows):
-        return jnp.concatenate([nat[species, 0, rows, :], nat[species, 1, rows, :]], axis=1)
-
-    for species in range(2):
-        placed = select_columns(natural(species, own_rows), own_choice[...])
-        for tile in range(3):
-            state[0, species, tile, pl.ds(TOP, ROWS), :] = placed[:, LANES * tile : LANES * (tile + 1)]
-
     pl.semaphore_wait(barrier, len(around) + PLANE - 1 + NZ - 1)
 
     moves = [
@@ -206,6 +192,21 @@
     ]
     for copy in copies:
         copy.start()
+
+    own_choice[...] = (iota((COLS, WIDE), 0) == woven(iota((COLS, WIDE), 1))).astype(BF16)
+    lane = iota((LANES, WIDE), 0)
+    side_column = jnp.where(lane < LANES // 2, COLS + lane, lane - LANES)
+    side_choice[...] = (side_column == woven(iota((LANES, WIDE), 1))).astype(BF16)
+    back_choice[...] = (woven(iota((WIDE, COLS), 0)) == iota((WIDE, COLS), 1)).astype(BF16)
+
+    def natural(species, rows):
+        return jnp.concatenate([nat[species, 0, rows, :], nat[species, 1, rows, :]], axis=1)
+
+    for species in range(2):
+        placed = select_columns(natural(species, own_rows), own_choice[...])
+        for tile in range(3):
+            state[0, species, tile, pl.ds(TOP, ROWS), :] = placed[:, LANES * tile : LANES * (tile + 1)]
+
     for copy in copies:
         copy.wait()
 
@@ -379,59 +380,75 @@
     shift = 0.01 * trace / SNAPS
     left = gram + jnp.where(diagonal, shift, 0.0)
     work = jnp.where(lane < SNAPS, left, lane_roll(gram, SNAPS))
-    for k in range(SNAPS):
-        pivot_row = work[k : k + 1, :]
-        scaled = pivot_row / work[k : k + 1, k : k + 1]
-        work = jnp.where(row == k, scaled, work - work[:, k : k + 1] * scaled)
+    size = 8
+    for k in range(0, SNAPS, size):
+        columns = [jnp.broadcast_to(work[:, k + j : k + j + 1], work.shape) for j in range(size)]
+        rows = [work[k + j : k + j + 1, :] for j in range(size)]
+        block = [[columns[j][k + i : k + i + 1, :] for j in range(size)] for i in range(size)]
+        for j in range(size):
+            inverse = 1.0 / block[j][j]
+            rows[j] = rows[j] * inverse
+            for m in range(j + 1, size):
+                block[j][m] = block[j][m] * inverse
+            for i in range(size):
+                if i != j:
+                    factor = block[i][j]
+                    rows[i] = rows[i] - factor * rows[j]
+                    for m in range(j + 1, size):
+                        block[i][m] = block[i][m] - factor * block[j][m]
+        for j in range(size):
+            work = work - columns[j] * rows[j]
+        for j in range(size):
+            work = jnp.where(row == k + j, rows[j], work)
     return lane_roll(work, -SNAPS)
 
 
-def filter_kernel(cent, packed, out, matrix_out, weights):
-    @pl.when(pl.program_id(0) == 0)
-    def _():
-        matrix = solve(packed[...])
-        matrix_out[...] = matrix[:, :SNAPS]
-        size = 8 * SNAPS
-        spread_rows = (iota((size, SNAPS), 0) // 8 == iota((size, SNAPS), 1)).astype(BF16)
-        spread_cols = (iota((SNAPS, size), 0) == iota((SNAPS, size), 1) // 8).astype(BF16)
-        turned = jnp.transpose(matrix)[:SNAPS, :].astype(BF16)
-        wide = jnp.dot(spread_rows, turned, preferred_element_type=F32).astype(BF16)
-        wide = jnp.dot(wide, spread_cols, preferred_element_type=F32)
-        same = iota((size, size), 0) % 8 == iota((size, size), 1) % 8
-        weights[...] = jnp.where(same, wide, 0.0).astype(BF16)
-
-    for part in range(cent.shape[0]):
-        block = jnp.dot(weights[...], cent[part], preferred_element_type=F32)
-        out[:, 0, pl.ds(8 * part, 8), :] = block.reshape(SNAPS, 8, COLS)
+def filter_kernel(cent, packed, out, matrix_out, stage, sem):
+    matrix = solve(packed[...])
+    matrix_out[...] = matrix[:, :SNAPS]
+    size = 8 * SNAPS
+    spread_rows = (iota((size, SNAPS), 0) // 8 == iota((size, SNAPS), 1)).astype(BF16)
+    spread_cols = (iota((SNAPS, size), 0) == iota((SNAPS, size), 1) // 8).astype(BF16)
+    turned = jnp.transpose(matrix)[:SNAPS, :].astype(BF16)
+    wide = jnp.dot(spread_rows, turned, preferred_element_type=F32).astype(BF16)
+    wide = jnp.dot(wide, spread_cols, preferred_element_type=F32)
+    same = iota((size, size), 0) % 8 == iota((size, size), 1) % 8
+    weights = jnp.where(same, wide, 0.0).astype(BF16)
+
+    parts = 2
+    copies = []
+    for chunk in range(TILES // parts):
+        first = chunk * parts
+        species = first // (ROWS // 8)
+        base = 8 * (first % (ROWS // 8))
+        for part in range(parts):
+            block = jnp.dot(weights, cent[first + part], preferred_element_type=F32)
+            stage[:, species, pl.ds(base + 8 * part, 8), :] = block.reshape(SNAPS, 8, COLS)
+        rows = pl.ds(base, 8 * parts)
+        copy = pltpu.make_async_copy(stage.at[:, species, rows, :], out.at[:, species, rows, :], sem.at[chunk])
+        copy.start()
+        copies.append(copy)
+    for copy in copies:
+        copy.wait()
 
 
 def apply_filter(cent, packed):
-    size = 8 * SNAPS
-    parts = 8
-    steps = TILES // parts
-    per_species = steps // 2
+    shape = (SNAPS, 2, ROWS, COLS)
     return pl.pallas_call(
         filter_kernel,
         name="apply_filter",
-        grid=(steps,),
-        out_shape=(
-            jax.ShapeDtypeStruct((SNAPS, 2, ROWS, COLS), F32),
-            jax.ShapeDtypeStruct((SNAPS, SNAPS), F32),
-        ),
-        in_specs=[
-            pl.BlockSpec((parts, size, COLS), lambda i: (i, 0, 0)),
-            pl.BlockSpec((8, LANES), lambda i: (0, 0)),
-        ],
-        out_specs=(
-            pl.BlockSpec((SNAPS, 1, 8 * parts, COLS), lambda i: (0, i // per_species, i % per_species, 0)),
-            pl.BlockSpec((SNAPS, SNAPS), lambda i: (0, 0)),
-        ),
-        scratch_shapes=[pltpu.VMEM((size, size), BF16)],
-        compiler_params=pltpu.CompilerParams(vmem_limit_bytes=12 * 1024 * 1024),
+        out_shape=(jax.ShapeDtypeStruct(shape, F32), jax.ShapeDtypeStruct((SNAPS, SNAPS), F32)),
+        in_specs=[pl.BlockSpec(memory_space=pltpu.VMEM), pl.BlockSpec(memory_space=pltpu.VMEM)],
+        out_specs=(pl.BlockSpec(memory_space=pltpu.HBM), pl.BlockSpec(memory_space=pltpu.VMEM)),
+        scratch_shapes=[pltpu.VMEM(shape, F32), pltpu.SemaphoreType.DMA((TILES // 2,))],
+        compiler_params=pltpu.CompilerParams(vmem_limit_bytes=24 * 1024 * 1024),
     )(cent, packed)
 
 
 def local(ramp, seed_mask, noise):
+    ramp, seed_mask, noise = [
+        pltpu.with_memory_space_constraint(value, pltpu.HBM) for value in (ramp, seed_mask, noise)
+    ]
     cent, packed = simulate(ramp, seed_mask, noise)
     return apply_filter(cent, packed)
 

time: 46.3 us -> 42.1 us (0.909)
  local copies, waits for them, and re-layouts: 2.5 us -> 0 us
  Pallas kernels: 43 us -> 41.3 us
    unnamed x6 -> x0, local copies, waits for them, and re-layouts: 2.5 us -> none
    pallas_call x1, Pallas kernels: 7.55 us -> 5.7 us  [apply_filter(): pl.pallas_call(filter_kernel, name='apply_filter', out_shape=(jax.ShapeDt...]
where the time goes in v3:
time: 42.1 us; the launch traced here: 41.9 us
  Pallas kernels  41.3 us (98%)
  between operations  0.64 us (2%)
    pallas_call x1, Pallas kernels, simulate(): pl.pallas_call(simulate_kernel, name='simulate', out_shape=(pltpu.VMEM((T...  35.6 us
    pallas_call x1, Pallas kernels, apply_filter(): pl.pallas_call(filter_kernel, name='apply_filter', out_shape=(jax.ShapeDt...  5.7 us

profile of v3, /device:TPU:1, one launch (start us, length us, event | category | flops | bytes accessed | tf_op | source)
XLA Modules:
  0.0 41.9 jit_solution(17281672292252063480)
XLA Ops:
  0.6 35.6 %simulate.1 = (bf16[32,256,256]{2,1,0:T(8,128)(2,1)S(1)}, f32[8,128]{1,0:T(8,128)S(1)}) custom-call(s32[32]{0:T(128)} %ramp.1, s32[128,256]{1,0:T(8,128)} %mask_hbm.1, f32[2,128,256]{2,1,0:T(8,128)} %noise_hbm.1), custom_call_target="tpu_custom_call" | custom-call | tf_op jit(solution)/shard_map/simulate/pallas_call | solution.py:331
  36.2 5.7 %apply_filter.1 = (f32[32,2,128,256]{3,2,1,0:T(8,128)}, f32[32,32]{1,0:T(8,128)}) custom-call(bf16[32,256,256]{2,1,0:T(8,128)(2,1)S(1)} %get-tuple-element.4.cent, f32[8,128]{1,0:T(8,128)S(1)} %get-tuple-element.5.packed), custom_call_target="tpu_custom_call" | custom-call | tf_op jit(solution)/shard_map/apply_filter/pallas_call | solution.py:437
